TPU v7x, 32 devices: a whole 2x2x4 slice. The times are simulated.
32 devices in a mesh: ctx: 8 (over y, x, core), ch: 4 (over z).
Axes of the slice: x: 2, y: 2, z: 4, core: 2. Of those that a mesh axis runs over, the one named last changes fastest.
Arguments:
- query: float32 [1024, 6144], P('ctx', 'ch'), may hold values from -6 to 6
- key_proj: float32 [1024, 6144], P('ctx', 'ch'), may hold values from -6 to 6
- value_proj: float32 [1024, 6144], P('ctx', 'ch'), may hold values from -6 to 6
- skip_gain: float32 [6144], P('ch'), may hold values from -4 to 4
- rates: float32 [384, 16], P('ch'), as said below
- residues: float32 [384, 16], P('ch')
- w_out: bfloat16 [6144, 8192], P('ch', 'ctx'), may hold values from -0.078125 to 0.078125
Outputs:
- projected_out: float32 [1024, 8192], P('ctx', 'ch')
Inputs may be any that keep to these rules, and one draw needn't show every extreme that they name: `rates`: each rate is positive, from 0.3 / 1024 up to 1 / 24.
All inputs are finite; a program needn't handle non-finite values.
Results may differ from a plain program's by a relative error of at most 0.0029.
Values may be sent and summed in bfloat16 or wider, within the bound.
A program may use at most 192 MiB of HBM per device.

v0:
```python
import jax
import jax.numpy as jnp
from jax import lax
from jax.sharding import PartitionSpec as P

SUB = 128


def shards(query, key_proj, value_proj, skip_gain, rates, residues, w_out):
    tok_rows, chan_count = query.shape
    filter_count, mode_count = rates.shape
    group_size = chan_count // filter_count
    sub_blocks = tok_rows // SUB
    highest = lax.Precision.HIGHEST
    kv_prod = key_proj * value_proj
    blocked = kv_prod.reshape(sub_blocks, SUB, filter_count, group_size).transpose(2, 3, 0, 1)
    lag_pos = jnp.arange(SUB, dtype=jnp.float32)
    lag_decay = jnp.exp(-rates[:, :, None] * lag_pos[None, None, :])
    filter_taps = jnp.einsum("fn,fnt->ft", residues, lag_decay, precision=highest)
    offset = jnp.arange(SUB)[None, :] - jnp.arange(SUB)[:, None]
    toeplitz = jnp.where(
        offset[None] >= 0, jnp.take(filter_taps, jnp.maximum(offset, 0), axis=1), 0.0
    )
    local_out = jnp.einsum("fgkj,fji->fgki", blocked, toeplitz, precision=highest)
    end_decay = jnp.exp(-rates[:, :, None] * (SUB - 1 - lag_pos)[None, None, :])
    states = jnp.einsum("fgkj,fnj->fgkn", blocked, end_decay, precision=highest)
    sub_index = jnp.arange(sub_blocks, dtype=jnp.float32)
    sub_gap = sub_index[:, None] - 1.0 - sub_index[None, :]
    within = jnp.where(
        sub_gap[None, None] >= 0,
        jnp.exp(-rates[:, :, None, None] * SUB * jnp.maximum(sub_gap, 0.0)[None, None]),
        0.0,
    )
    prefix = jnp.einsum("fnkl,fgln->fgkn", within, states, precision=highest)
    tail_decay = jnp.exp(-rates[:, :, None] * SUB * (sub_blocks - 1 - sub_index)[None, None, :])
    own_state = jnp.einsum("fnk,fgkn->fgn", tail_decay, states, precision=highest)
    position = lax.axis_index("ctx")
    block_piece = lax.all_gather(own_state[None], "ctx", axis=0, tiled=True)
    source_rank = jnp.arange(block_piece.shape[0])
    rank_gap = (position - 1 - source_rank).astype(jnp.float32)
    weight = jnp.where(
        rank_gap[:, None, None] >= 0,
        jnp.exp(-rates[None] * tok_rows * jnp.maximum(rank_gap, 0.0)[:, None, None]),
        0.0,
    )
    incoming = jnp.einsum("jfn,jfgn->fgn", weight, block_piece, precision=highest)
    entry_decay = jnp.exp(-rates[:, :, None] * SUB * sub_index[None, None, :])
    carried = (
        prefix + incoming[:, :, None, :] * jnp.transpose(entry_decay, (0, 2, 1))[:, None, :, :]
    )
    out_decay = residues[:, :, None] * jnp.exp(-rates[:, :, None] * (lag_pos + 1.0)[None, None, :])
    cross_out = jnp.einsum("fgkn,fni->fgki", carried, out_decay, precision=highest)
    conv_out = (local_out + cross_out).transpose(2, 3, 0, 1).reshape(tok_rows, chan_count)
    hidden = (query * (conv_out + skip_gain[None, :] * kv_prod)).astype(jnp.bfloat16)
    partial_out = jnp.dot(
        hidden, lax.all_gather(w_out, "ctx", axis=1, tiled=True), preferred_element_type=jnp.float32
    )
    return lax.psum_scatter(partial_out, "ch", scatter_dimension=1, tiled=True)


def solution(mesh):
    placed = (
        P("ctx", "ch"),
        P("ctx", "ch"),
        P("ctx", "ch"),
        P("ch"),
        P("ch", None),
        P("ch", None),
        P("ch", "ctx"),
    )
    return jax.shard_map(
        shards, mesh=mesh, in_specs=placed, out_specs=P("ctx", "ch"), check_vma=False
    )
```

profile of v0, /device:TPU:3, one launch (start us, length us, event | category | flops | bytes accessed | tf_op | source)
XLA Modules:
  0.0 253.2 jit_solution(7362462676393946079)
XLA Ops:
  6.5 0.0 all-gather.3.cloned.1.call-start
  6.5 0.7 all-gather.3.cloned.1.call-update
  7.3 0.0 reduce-scatter.2.cloned.1.call-start
  7.3 0.7 broadcast_multiply_fusion
  8.0 0.1 copy.27
  8.1 1.4 copy.25
  9.5 1.4 copy.26
  10.9 0.1 copy.29
  11.0 0.1 mul.51
  11.1 1.4 fusion.18
  12.6 0.3 multiply_bitcast_fusion
  12.8 0.3 copy.30
  13.1 0.1 copy.31
  13.2 54.2 %all-gather = f32[768,16,16]{2,1,0:T(8,128)S(1)} all-gather(f32[96,16,16]{2,1,0:T(8,128)S(1)} %copy.30), channel_id=2, replica_groups=mesh['ctx'=8,'ch'=4] {'ctx'}, dimensions={0}, use_global_device_ids=true | all-gather | bytes 884736 | tf_op jit(solution)/shard_map/all_gather | solution.py:38
  67.4 0.0 copy-start.1
  67.4 0.1 select_bitcast_fusion
  67.6 0.9 multiply_reduce_fusion
  68.5 0.3 copy.46
  68.8 0.0 copy-done.1
  68.8 0.1 copy.48
  68.9 0.5 multiply_reduce_fusion.1
  69.4 0.1 copy.38
  69.5 54.5 %gather_fusion = f32[16384,96]{1,0:T(8,128)} fusion(f32[96,128]{0,1:T(8,128)S(1)} %copy.38, s32[16384]{0:T(1024)S(1)} %bitcast_clamp_fusion), kind=kCustom, calls=%fused_computation | custom fusion | bytes 12648448 | tf_op jit(solution)/shard_map/jit(_take)/gather | solution.py:22
  124.0 8.6 %copy.28 = f32[128,128,96]{1,0,2:T(8,128)} copy(f32[128,128,96]{2,1,0:T(8,128)} %bitcast.49) | data formatting | bytes 12582912 | tf_op jit(solution)/shard_map/jit(_take)/gather | solution.py:22
  132.6 0.0 copy-start
  132.6 1.4 copy.34
  134.1 7.6 %fusion = f32[96,16,128]{2,1,0:T(8,128)S(1)} fusion(f32[96,16,128]{2,1,0:T(8,128)S(1)} %bitcast.52, f32[128,128,96]{1,0,2:T(8,128)} %copy.28, pred[128,128]{1,0:T(8,128)(4,1)S(1)} %get-tuple-element.9, pred[128,128]{1,0:T(8,128)(4,1)S(1)} %get-tuple-element.8), kind=kOutput, calls=%fused_computation.1 | convolution fusion | flops 305135616 | bytes 7897088 | tf_op jit(solution)/shard_map/fgkj,fji->fgki/dot_general | solution.py:24
  141.7 2.1 convolution_add_fusion
  143.8 0.0 copy-done
  143.8 0.3 fusion.9
  144.1 11.9 %all-gather.3.cloned.1.call-done = bf16[1536,8192]{1,0:T(8,128)(2,1)} async-done(((bf16[1536,1024]{1,0:T(8,128)(2,1)}), bf16[1536,8192]{1,0:T(8,128)(2,1)}) %all-gather.3.cloned.1.call-update) | async-done | bytes 25165840 | tf_op jit(solution)/shard_map/all_gather | solution.py:56
  156.0 13.7 %fusion.32 = f32[128,8192]{1,0:T(8,128)} fusion(bf16[128,1536]{0,1:T(8,128)(2,1)S(1)} %fusion.9, bf16[1536,8192]{1,0:T(8,128)(2,1)} %all-gather.3.cloned.1.call-done), kind=kOutput, calls=%fused_computation.49 | convolution fusion | flops 3221225472 | bytes 29753344 | tf_op jit(solution)/shard_map/dot_general | solution.py:55
  169.8 0.0 reduce-scatter.2.cloned.1.call-update
  169.8 76.5 %reduce-scatter.2.cloned.1.call-done = f32[128,2048]{1,0:T(8,128)} async-done(((f32[128,8192]{1,0:T(8,128)}), f32[128,2048]{1,0:T(8,128)}) %reduce-scatter.2.cloned.1.call-update) | async-done | bytes 1048592 | tf_op jit(solution)/shard_map/reduce_scatter | solution.py:58
  (6 shorter events, 0.1 us)
Async XLA Ops:
  6.5 149.5 %all-gather.3.cloned.1.call-start = ((), (), s32[]{:S(2)}) async-start(), calls=%async_computation.1 | async-start | bytes 28311552 | tf_op jit(solution)/shard_map/all_gather | solution.py:56
  7.3 239.1 %reduce-scatter.2.cloned.1.call-start = ((), (), s32[]{:S(2)}) async-start(), calls=%async_computation.2 | async-start | bytes 5242880 | tf_op jit(solution)/shard_map/reduce_scatter | solution.py:58
  67.4 1.3 copy-start.1
  132.6 11.1 %copy-start = (f32[1536]{0:T(1024)S(1)}, f32[1536]{0:T(1024)}, u32[]{:S(2)}) copy-start(f32[1536]{0:T(1024)} %param.10) | copy-start | bytes 18436
Sparse Core Ops, SparseCore 0:
  9.3 146.7 all-gather.2
  169.9 76.3 reduce-scatter.1
where the time goes:
time: 255 us; the launch traced here: 253 us
  waiting for transfers between devices  89.2 us (35%)
  local copies, waits for them, and re-layouts  68.3 us (27%)
  blocking collectives  54.2 us (21%)
  matrix products  24.8 us (10%)
  between operations  13.6 us (5%)
  other arithmetic  2.98 us (1%)
    reduce_scatter x1, waiting for transfers between devices, shards(): return lax.psum_scatter(partial_out, 'ch', scatter_dimension=1, tiled=True)  76.5 us
    gather x2, local copies, waits for them, and re-layouts, shards(): jnp.take(filter_taps, jnp.maximum(offset, 0), axis=1)  63.1 us
    all_gather x1, blocking collectives, shards(): block_piece = lax.all_gather(own_state[None], 'ctx', axis=0, tiled=True)  54.2 us
    dot_general x1, matrix products, shards(): jnp.dot(hidden, lax.all_gather(w_out, 'ctx', axis=1, tiled=True), preferr...  13.7 us
    all_gather x1, waiting for transfers between devices, shards(): lax.all_gather(w_out, 'ctx', axis=1, tiled=True)  11.9 us
    dot_general x1, matrix products, shards(): jnp.einsum('fgkj,fji->fgki', blocked, toeplitz, precision=highest)  7.6 us
  transfers between devices with their start and end apart: 2, of which 2 were waited for; matrix products, arithmetic and copies ran while one was open for 33% of the time, Pallas kernels for 0%

commit v1 on v0

v1 whole, which is shorter than its diff:
```python
import functools

import jax
import jax.numpy as jnp
from jax import lax
from jax.experimental import pallas as pl
from jax.experimental.pallas import tpu as pltpu
from jax.sharding import PartitionSpec as P

HIGHEST = lax.Precision.HIGHEST
LANES = 128


def dot_nt(a, b):
    return lax.dot_general(
        a, b, (((1,), (1,)), ((), ())), precision=HIGHEST, preferred_element_type=jnp.float32
    )


def dot_tn(a, b):
    return lax.dot_general(
        a, b, (((0,), (0,)), ((), ())), precision=HIGHEST, preferred_element_type=jnp.float32
    )


def dot_nn(a, b):
    return jnp.dot(a, b, precision=HIGHEST, preferred_element_type=jnp.float32)


def own_filter(modes, rows):
    shape = (LANES // modes, rows, LANES)
    return lax.broadcasted_iota(jnp.int32, shape, 2) // modes == lax.broadcasted_iota(
        jnp.int32, shape, 0
    )


def local_kernel(modes, key_ref, value_ref, rate_ref, res_ref, state_ref, conv_ref):
    tok = key_ref.shape[0]
    filters = LANES // modes
    kv = key_ref[...] * value_ref[...]
    rate = rate_ref[...]
    pos = lax.broadcasted_iota(jnp.int32, (tok, LANES), 0).astype(jnp.float32)
    end = jnp.exp(-rate * (tok - 1.0 - pos))
    full = dot_tn(end, kv).reshape(filters, modes, LANES)
    state_ref[...] = jnp.sum(jnp.where(own_filter(modes, modes), full, 0.0), axis=0)
    centre = pos - tok / 2.0
    rise = res_ref[...] * jnp.exp(rate * centre)
    fall = jnp.exp(-rate * centre)
    mine = own_filter(modes, tok)
    falls = jnp.where(mine, fall[None], 0.0).reshape(filters * tok, LANES)
    taps = dot_nt(falls, rise).reshape(filters, tok, tok)
    shape = (filters, tok, tok)
    causal = lax.broadcasted_iota(jnp.int32, shape, 1) >= lax.broadcasted_iota(jnp.int32, shape, 2)
    taps = jnp.where(causal, taps, 0.0).reshape(filters * tok, tok)
    out = dot_nn(taps, kv).reshape(filters, tok, LANES)
    conv_ref[...] = jnp.sum(jnp.where(mine, out, 0.0), axis=0)


def gate_kernel(
    modes, ctx_count, query_ref, key_ref, value_ref, skip_ref, rate_ref, res_ref, conv_ref,
    rates_nc_ref, states_ref, hidden_ref
):
    tok = key_ref.shape[0]
    filters = LANES // modes
    me = lax.axis_index("ctx")
    carry = jnp.zeros((modes, LANES), jnp.float32)
    decay = jnp.exp(-rates_nc_ref[...] * float(tok))

    def add(j, carry):
        return jnp.where(j < me, carry * decay + states_ref[j], carry)

    carry = lax.fori_loop(0, ctx_count, add, carry)
    spread = jnp.where(
        own_filter(modes, modes), jnp.broadcast_to(carry[None], (filters, modes, LANES)), 0.0
    ).reshape(LANES, LANES)
    pos = lax.broadcasted_iota(jnp.int32, (tok, LANES), 0).astype(jnp.float32)
    out_decay = res_ref[...] * jnp.exp(-rate_ref[...] * (pos + 1.0))
    kv = key_ref[...] * value_ref[...]
    conv = conv_ref[...] + dot_nn(out_decay, spread)
    hidden_ref[...] = (query_ref[...] * (conv + skip_ref[...] * kv)).astype(jnp.bfloat16)


def shards(query, key_proj, value_proj, skip_gain, rates, residues, w_out):
    tok, chan = query.shape
    filters, modes = rates.shape
    width = chan // filters
    ctx_count = lax.axis_size("ctx")
    ch_count = lax.axis_size("ch")
    rate_row = rates.reshape(1, filters * modes)
    res_row = residues.reshape(1, filters * modes)
    rates_nc = jnp.repeat(rates.T, width, axis=1)
    groups = chan // LANES
    wide = pl.BlockSpec((tok, LANES), lambda g: (0, g))
    row = pl.BlockSpec((1, LANES), lambda g: (0, g))
    small = pl.BlockSpec((modes, LANES), lambda g: (0, g))
    state, conv = pl.pallas_call(
        functools.partial(local_kernel, modes),
        grid=(groups,),
        in_specs=[wide, wide, row, row],
        out_specs=[small, wide],
        out_shape=[
            jax.ShapeDtypeStruct((modes, chan), jnp.float32),
            jax.ShapeDtypeStruct((tok, chan), jnp.float32),
        ],
    )(key_proj, value_proj, rate_row, res_row)
    states = lax.all_gather(state, "ctx", axis=0)
    hidden = pl.pallas_call(
        functools.partial(gate_kernel, modes, ctx_count),
        grid=(groups,),
        in_specs=[
            wide, wide, wide, row, row, row, wide, small,
            pl.BlockSpec((ctx_count, modes, LANES), lambda g: (0, 0, g)),
        ],
        out_specs=wide,
        out_shape=jax.ShapeDtypeStruct((tok, chan), jnp.bfloat16),
    )(query, key_proj, value_proj, skip_gain[None], rate_row, res_row, conv, rates_nc, states)
    hidden_all = lax.all_gather(hidden, "ctx", axis=0, tiled=True)
    part = jnp.dot(hidden_all, w_out, preferred_element_type=jnp.float32).astype(jnp.bfloat16)
    part = part.reshape(ctx_count, tok, w_out.shape[1])
    part = lax.all_to_all(part, "ctx", split_axis=0, concat_axis=0)
    part = part.reshape(ch_count, ctx_count // ch_count, tok, w_out.shape[1])
    part = lax.all_to_all(part, "ch", split_axis=0, concat_axis=0)
    total = jnp.sum(part.astype(jnp.float32), axis=0)
    return total.transpose(1, 0, 2).reshape(tok, -1)


def solution(mesh):
    placed = (
        P("ctx", "ch"),
        P("ctx", "ch"),
        P("ctx", "ch"),
        P("ch"),
        P("ch", None),
        P("ch", None),
        P("ch", "ctx"),
    )
    return jax.shard_map(
        shards, mesh=mesh, in_specs=placed, out_specs=P("ctx", "ch"), check_vma=False
    )
```

time: 255 us -> 194 us (0.76)
  waiting for transfers between devices: 89.2 us -> 33.6 us
  local copies, waits for them, and re-layouts: 68.3 us -> 13.5 us
  blocking collectives: 54.2 us -> 91.6 us
  Pallas kernels: 0 us -> 31.7 us
  matrix products: 24.8 us -> 5.49 us
    all_to_all x0 -> x2, blocking collectives: none -> 79.7 us  [the longest x1 51.8 us: shards(): part = lax.all_to_all(part, 'ch', split_axis=0, concat_axis=0)]
    reduce_scatter x1 -> x0, waiting for transfers between devices: 76.5 us -> none  [shards(): return lax.psum_scatter(partial_out, 'ch', scatter_dimension=1, tiled=True)]
    gather x2 -> x0, local copies, waits for them, and re-layouts: 63.1 us -> none  [shards(): jnp.take(filter_taps, jnp.maximum(offset, 0), axis=1)]
    all_gather x1, blocking collectives: 54.2 us -> 11.9 us  [shards(): states = lax.all_gather(state, 'ctx', axis=0)]
    pallas_call x0 -> x2, Pallas kernels: none -> 31.7 us  [the longest x1 22.7 us: shards(): pl.pallas_call(functools.partial(local_kernel, modes), grid=(groups,), in...]
    all_gather x1, waiting for transfers between devices: 11.9 us -> 33.6 us  [shards(): hidden_all = lax.all_gather(hidden, 'ctx', axis=0, tiled=True)]
    dot_general x4 -> x1, matrix products: 24.8 us -> 5.49 us  [shards(): jnp.dot(hidden_all, w_out, preferred_element_type=jnp.float32)]
    reshape x0 -> x4, local copies, waits for them, and re-layouts: none -> 6.1 us  [the longest x1 2.53 us: shards(): return total.transpose(1, 0, 2).reshape(tok, -1)]
  transfers between devices with their start and end apart: 2 -> 1, of which waited for: 2 -> 1; matrix products, arithmetic and copies ran while one was open for 33% -> 0% of each run, Pallas kernels for 0% -> 0%
where the time goes in v1:
time: 194 us; the launch traced here: 191 us
  blocking collectives  91.6 us (47%)
  waiting for transfers between devices  33.6 us (17%)
  Pallas kernels  31.7 us (16%)
  local copies, waits for them, and re-layouts  13.5 us (7%)
  between operations  13.4 us (7%)
  matrix products  5.49 us (3%)
    all_to_all x1, blocking collectives, shards(): part = lax.all_to_all(part, 'ch', split_axis=0, concat_axis=0)  51.8 us
    all_gather x1, waiting for transfers between devices, shards(): hidden_all = lax.all_gather(hidden, 'ctx', axis=0, tiled=True)  33.6 us
    all_to_all x1, blocking collectives, shards(): part = lax.all_to_all(part, 'ctx', split_axis=0, concat_axis=0)  27.9 us
    pallas_call x1, Pallas kernels, shards(): pl.pallas_call(functools.partial(local_kernel, modes), grid=(groups,), in...  22.7 us
    all_gather x1, blocking collectives, shards(): states = lax.all_gather(state, 'ctx', axis=0)  11.9 us
    pallas_call x1, Pallas kernels, shards(): pl.pallas_call(functools.partial(gate_kernel, modes, ctx_count), grid=(gr...  9.08 us
    dot_general x1, matrix products, shards(): jnp.dot(hidden_all, w_out, preferred_element_type=jnp.float32)  5.49 us
  transfers between devices with their start and end apart: 1, of which 1 were waited for; matrix products, arithmetic and copies ran while one was open for 0% of the time, Pallas kernels for 0%

profile of v1, /device:TPU:3, one launch (start us, length us, event | category | flops | bytes accessed | tf_op | source)
XLA Modules:
  0.0 190.7 jit_solution(5505469806628715310)
XLA Ops:
  6.5 0.0 copy-start
  6.5 0.0 all-gather.3.cloned.1.call-start
  6.5 1.4 broadcast_in_dim.6.skip_ref
  8.0 0.8 copy.15
  8.8 0.7 reshape.19.res_ref
  9.5 0.8 copy.14
  10.3 0.7 reshape.18.rate_ref
  10.9 1.8 broadcast_in_dim.7
  12.8 2.2 %reshape.20.rates_nc_ref = f32[16,1536]{1,0:T(8,128)} reshape(f32[16,96,16]{2,1,0:T(8,128)} %broadcast_in_dim.7) | data formatting | bytes 196608 | tf_op jit(solution)/shard_map/reshape | solution.py:91
  15.0 22.7 %shard_map.73 = (f32[16,1536]{1,0:T(8,128)}, f32[128,1536]{1,0:T(8,128)}) custom-call(f32[128,1536]{1,0:T(8,128)} %key_ref.3, f32[128,1536]{1,0:T(8,128)} %value_ref.3, f32[1,1536]{1,0:T(1,128)} %reshape.18.rate_ref, f32[1,1536]{1,0:T(1,128)} %reshape.19.res_ref), custom_call_target="tpu_custom_call" | custom-call | tf_op jit(solution)/shard_map/pallas_call | solution.py:96
  37.6 11.9 %all-gather = f32[128,1536]{1,0:T(8,128)} all-gather(f32[16,1536]{1,0:T(8,128)} %get-tuple-element.8), channel_id=2, replica_groups=mesh['ctx'=8,'ch'=4] {'ctx'}, dimensions={0}, use_global_device_ids=true | all-gather | bytes 884736 | tf_op jit(solution)/shard_map/all_gather | solution.py:106
  49.5 9.1 %shard_map.74 = bf16[128,1536]{1,0:T(8,128)(2,1)} custom-call(f32[128,1536]{1,0:T(8,128)} %query_ref.1, f32[128,1536]{1,0:T(8,128)} %key_ref.3, f32[128,1536]{1,0:T(8,128)} %value_ref.3, f32[1,1536]{1,0:T(1,128)} %broadcast_in_dim.6.skip_ref, f32[1,1536]{1,0:T(1,128)} %reshape.18.rate_ref, f32[1,1536]{1,0:T(1,128)} %reshape.19.res_ref, ...), custom_call_target="tpu_custom_call" | custom-call | tf_op jit(solution)/shard_map/pallas_call | solution.py:107
  58.6 0.0 all-gather.3.cloned.1.call-update
  58.6 33.6 %all-gather.3.cloned.1.call-done = bf16[1024,1536]{1,0:T(8,128)(2,1)} async-done(((bf16[128,1536]{1,0:T(8,128)(2,1)}), bf16[1024,1536]{1,0:T(8,128)(2,1)}) %all-gather.3.cloned.1.call-update) | async-done | bytes 3145744 | tf_op jit(solution)/shard_map/all_gather | solution.py:117
  92.3 0.0 copy-done
  92.3 5.5 %convolution_convert_fusion = bf16[1024,1024]{1,0:T(8,128)(2,1)S(1)} fusion(bf16[1024,1536]{1,0:T(8,128)(2,1)} %all-gather.3.cloned.1.call-done, bf16[1536,1024]{1,0:T(8,128)(2,1)S(1)} %copy-done), kind=kOutput, calls=%fused_computation.1 | convolution fusion | flops 3222274048 | bytes 8388608 | tf_op jit(solution)/shard_map/dot_general | solution.py:118
  97.8 27.9 %all_to_all.10 = bf16[8,128,1024]{2,1,0:T(8,128)(2,1)S(1)} all-to-all(bf16[8,128,1024]{2,1,0:T(8,128)(2,1)S(1)} %bitcast.12), channel_id=1, replica_groups=mesh['ctx'=8,'ch'=4] {'ctx'}, dimensions={0} | all-to-all | bytes 4194304 | tf_op jit(solution)/shard_map/all_to_all | solution.py:120
  125.7 51.8 %all_to_all.11 = bf16[4,2,128,1024]{3,2,1,0:T(8,128)(2,1)S(1)} all-to-all(bf16[4,2,128,1024]{3,2,1,0:T(8,128)(2,1)S(1)} %bitcast.8), channel_id=1, replica_groups=mesh['ctx'=8,'ch'=4] {'ch'}, dimensions={0} | all-to-all | bytes 4194304 | tf_op jit(solution)/shard_map/all_to_all | solution.py:122
  177.5 1.4 convert_reduce_fusion
  178.8 2.5 %copy.16 = f32[128,2,1024]{0,2,1:T(8,128)} copy(f32[128,2,1024]{2,0,1:T(8,128)} %bitcast.9) | data formatting | bytes 2097152 | tf_op jit(solution)/shard_map/transpose | solution.py:124
  181.4 2.5 %copy.17 = f32[128,2048]{1,0:T(8,128)} copy(f32[128,2048]{0,1:T(8,128)} %bitcast.10) | data formatting | bytes 2097152 | tf_op jit(solution)/shard_map/reshape | solution.py:124
Async XLA Ops:
  6.5 85.7 %copy-start = (bf16[1536,1024]{1,0:T(8,128)(2,1)S(1)}, bf16[1536,1024]{1,0:T(8,128)(2,1)}, u32[]{:S(2)}) copy-start(bf16[1536,1024]{1,0:T(8,128)(2,1)} %param.13) | copy-start | bytes 9437188
  6.5 85.7 %all-gather.3.cloned.1.call-start = ((), (), s32[]{:S(2)}) async-start(), calls=%async_computation.2 | async-start | bytes 3538944 | tf_op jit(solution)/shard_map/all_gather | solution.py:117
Sparse Core Ops, SparseCore 0:
  58.8 33.4 all-gather.2

commit v2 on v1

--- a/solution.py
+++ b/solution.py
@@ -7,24 +7,33 @@
 from jax.experimental.pallas import tpu as pltpu
 from jax.sharding import PartitionSpec as P
 
-HIGHEST = lax.Precision.HIGHEST
 LANES = 128
 
 
+MESH = pl.DeviceIdType.MESH
+
+
+def split3(a, b, dims):
+    a_hi, b_hi = a.astype(jnp.bfloat16), b.astype(jnp.bfloat16)
+    a_lo = (a - a_hi.astype(jnp.float32)).astype(jnp.bfloat16)
+    b_lo = (b - b_hi.astype(jnp.float32)).astype(jnp.bfloat16)
+
+    def one(x, y):
+        return lax.dot_general(x, y, (dims, ((), ())), preferred_element_type=jnp.float32)
+
+    return one(a_hi, b_hi) + (one(a_hi, b_lo) + one(a_lo, b_hi))
+
+
 def dot_nt(a, b):
-    return lax.dot_general(
-        a, b, (((1,), (1,)), ((), ())), precision=HIGHEST, preferred_element_type=jnp.float32
-    )
+    return split3(a, b, ((1,), (1,)))
 
 
 def dot_tn(a, b):
-    return lax.dot_general(
-        a, b, (((0,), (0,)), ((), ())), precision=HIGHEST, preferred_element_type=jnp.float32
-    )
+    return split3(a, b, ((0,), (0,)))
 
 
 def dot_nn(a, b):
-    return jnp.dot(a, b, precision=HIGHEST, preferred_element_type=jnp.float32)
+    return split3(a, b, ((1,), (0,)))
 
 
 def own_filter(modes, rows):
@@ -78,6 +87,158 @@
     kv = key_ref[...] * value_ref[...]
     conv = conv_ref[...] + dot_nn(out_decay, spread)
     hidden_ref[...] = (query_ref[...] * (conv + skip_ref[...] * kv)).astype(jnp.bfloat16)
+
+
+def exchange_kernel(
+    n, nch, hidden_ref, w_ref, out_ref, held, part, mine, others,
+    own_send, pass_send, h_recv, p_send, p_recv, z_send, z_recv
+):
+    me, my_ch = lax.axis_index("ctx"), lax.axis_index("ch")
+    tok = hidden_ref.shape[0]
+    cols = w_ref.shape[1]
+    per = n // nch
+    chips = n // 2
+    tile = min(cols, 256)
+
+    def sibling(i):
+        return i + 1 - 2 * lax.rem(i, 2)
+
+    sib = sibling(me)
+
+    barrier = pltpu.get_barrier_semaphore()
+
+    def greet_ctx(d, c):
+        pl.semaphore_signal(
+            barrier, inc=1, device_id={"ctx": lax.rem(me + d, n)}, device_id_type=MESH
+        )
+        return c
+
+    lax.fori_loop(1, n, greet_ctx, 0)
+    for d in range(1, nch):
+        pl.semaphore_signal(
+            barrier, inc=1, device_id={"ch": lax.rem(my_ch + d, nch)}, device_id_type=MESH
+        )
+    pl.semaphore_wait(barrier, n + nch - 2)
+
+    def own_copy(d, peer):
+        return pltpu.make_async_remote_copy(
+            src_ref=hidden_ref, dst_ref=held.at[me], send_sem=own_send.at[d],
+            recv_sem=h_recv.at[me], device_id={"ctx": peer}, device_id_type=MESH,
+        )
+
+    def pass_copy(d, src):
+        return pltpu.make_async_remote_copy(
+            src_ref=held.at[src], dst_ref=held.at[src], send_sem=pass_send.at[d],
+            recv_sem=h_recv.at[src], device_id={"ctx": sib}, device_id_type=MESH,
+        )
+
+    def part_copy(b, t, src):
+        return pltpu.make_async_remote_copy(
+            src_ref=part.at[t], dst_ref=mine.at[src], send_sem=p_send.at[b],
+            recv_sem=p_recv.at[src], device_id={"ctx": t}, device_id_type=MESH,
+        )
+
+    def ch_copy(i, to, src_ch):
+        slot = lax.rem(i, per)
+        return pltpu.make_async_remote_copy(
+            src_ref=mine.at[i], dst_ref=others.at[src_ch, slot], send_sem=z_send.at[i],
+            recv_sem=z_recv.at[src_ch, slot], device_id={"ch": to}, device_id_type=MESH,
+        )
+
+    own_copy(0, sib).start()
+
+    def send_own(d, c):
+        own_copy(d, lax.rem(me + 2 * d, n)).start()
+        return c
+
+    lax.fori_loop(1, chips, send_own, 0)
+    held[me] = hidden_ref[...]
+
+    def block_of(b, sign):
+        base = lax.rem(me + sign * 2 * (b // 2) + 2 * n, n)
+        odd = lax.rem(b, 2)
+        return base + odd * (1 - 2 * lax.rem(base, 2))
+
+    def forward(b):
+        i = block_of(b, 1)
+
+        @pl.when(b > 0)
+        def _():
+            part_copy(b, me, i).wait_recv()
+
+        to = i // per
+
+        @pl.when(to != my_ch)
+        def _():
+            ch_copy(i, to, my_ch).start()
+
+    def step(b, c):
+        t = block_of(b, -1)
+
+        @pl.when(b > 0)
+        def _():
+            pass_copy(0, t).wait_recv()
+
+        @pl.when(jnp.logical_and(b > 0, lax.rem(b, 2) == 0))
+        def _():
+            pass_copy(b // 2, t).start()
+
+        for k in range(cols // tile):
+            at = pl.ds(k * tile, tile)
+            part[t, :, at] = jnp.dot(
+                held[t], w_ref[:, at], preferred_element_type=jnp.float32
+            ).astype(jnp.bfloat16)
+
+        @pl.when(b > 0)
+        def _():
+            part_copy(b, t, me).start()
+
+        @pl.when(b == 0)
+        def _():
+            mine[me] = part[me]
+
+        @pl.when(b > 1)
+        def _():
+            forward(b - 2)
+
+        return c
+
+    lax.fori_loop(0, n, step, 0)
+    forward(n - 2)
+    forward(n - 1)
+
+    for slot in range(per):
+        i = my_ch * per + slot
+        total = mine[i].astype(jnp.float32)
+        for d in range(1, nch):
+            src_ch = lax.rem(my_ch + d, nch)
+            ch_copy(i, src_ch, src_ch).wait_recv()
+            total = total + others[src_ch, slot].astype(jnp.float32)
+        out_ref[:, slot * cols : (slot + 1) * cols] = total
+
+    own_copy(0, sib).wait_send()
+
+    def drain_own(d, c):
+        own_copy(d, sib).wait_send()
+        pass_copy(d, me).wait_send()
+        return c
+
+    lax.fori_loop(1, chips, drain_own, 0)
+
+    def drain_part(b, c):
+        part_copy(b, block_of(b, -1), me).wait_send()
+        return c
+
+    lax.fori_loop(1, n, drain_part, 0)
+
+    def drain_ch(i, c):
+        @pl.when(i // per != my_ch)
+        def _():
+            ch_copy(i, i // per, my_ch).wait_send()
+
+        return c
+
+    lax.fori_loop(0, n, drain_ch, 0)
 
 
 def shards(query, key_proj, value_proj, skip_gain, rates, residues, w_out):
@@ -114,14 +275,31 @@
         out_specs=wide,
         out_shape=jax.ShapeDtypeStruct((tok, chan), jnp.bfloat16),
     )(query, key_proj, value_proj, skip_gain[None], rate_row, res_row, conv, rates_nc, states)
-    hidden_all = lax.all_gather(hidden, "ctx", axis=0, tiled=True)
-    part = jnp.dot(hidden_all, w_out, preferred_element_type=jnp.float32).astype(jnp.bfloat16)
-    part = part.reshape(ctx_count, tok, w_out.shape[1])
-    part = lax.all_to_all(part, "ctx", split_axis=0, concat_axis=0)
-    part = part.reshape(ch_count, ctx_count // ch_count, tok, w_out.shape[1])
-    part = lax.all_to_all(part, "ch", split_axis=0, concat_axis=0)
-    total = jnp.sum(part.astype(jnp.float32), axis=0)
-    return total.transpose(1, 0, 2).reshape(tok, -1)
+    cols = w_out.shape[1]
+    per = ctx_count // ch_count
+    block = (tok, cols)
+    return pl.pallas_call(
+        functools.partial(exchange_kernel, ctx_count, ch_count),
+        in_specs=[pl.BlockSpec(memory_space=pltpu.VMEM)] * 2,
+        out_specs=pl.BlockSpec(memory_space=pltpu.VMEM),
+        out_shape=jax.ShapeDtypeStruct((tok, per * cols), jnp.float32),
+        scratch_shapes=[
+            pltpu.VMEM((ctx_count, tok, chan), jnp.bfloat16),
+            pltpu.VMEM((ctx_count, *block), jnp.bfloat16),
+            pltpu.VMEM((ctx_count, *block), jnp.bfloat16),
+            pltpu.VMEM((ch_count, per, *block), jnp.bfloat16),
+            pltpu.SemaphoreType.DMA((ctx_count // 2,)),
+            pltpu.SemaphoreType.DMA((ctx_count // 2,)),
+            pltpu.SemaphoreType.DMA((ctx_count,)),
+            pltpu.SemaphoreType.DMA((ctx_count,)),
+            pltpu.SemaphoreType.DMA((ctx_count,)),
+            pltpu.SemaphoreType.DMA((ctx_count,)),
+            pltpu.SemaphoreType.DMA((ch_count, per)),
+        ],
+        compiler_params=pltpu.CompilerParams(
+            collective_id=0, has_side_effects=True, vmem_limit_bytes=56 << 20
+        ),
+    )(hidden, w_out)
 
 
 def solution(mesh):

time: 194 us -> 129 us (0.66); the launches traced: 191 us -> 128 us
  blocking collectives: 91.6 us -> 11.9 us
  Pallas kernels: 31.7 us -> 107 us
  waiting for transfers between devices: 33.6 us -> 0 us
  between operations: 13.4 us -> 0.02 us
  matrix products: 5.49 us -> 0 us
  local copies, waits for them, and re-layouts: 13.5 us -> 8.54 us
    pallas_call x0 -> x1, Pallas kernels: none -> 84.2 us  [shards(): pl.pallas_call(functools.partial(exchange_kernel, ctx_count, ch_count), i...]
    all_to_all x2 -> x0, blocking collectives: 79.7 us -> none  [the longest x1 51.8 us: shards(): part = lax.all_to_all(part, 'ch', split_axis=0, concat_axis=0)]
    all_gather x1 -> x0, waiting for transfers between devices: 33.6 us -> none  [shards(): hidden_all = lax.all_gather(hidden, 'ctx', axis=0, tiled=True)]
    pallas_call x1, Pallas kernels: 22.7 us -> 14.4 us  [shards(): pl.pallas_call(functools.partial(local_kernel, modes), grid=(groups,), in...]
    dot_general x1 -> x0, matrix products: 5.49 us -> none  [shards(): jnp.dot(hidden_all, w_out, preferred_element_type=jnp.float32)]
    transpose x1 -> x0, local copies, waits for them, and re-layouts: 2.53 us -> none  [shards(): return total.transpose(1, 0, 2).reshape(tok, -1)]
    reshape x1 -> x0, local copies, waits for them, and re-layouts: 2.53 us -> none  [shards(): return total.transpose(1, 0, 2).reshape(tok, -1)]
    unnamed x4 -> x3, local copies, waits for them, and re-layouts: 1.58 us -> 3.87 us
  transfers between devices with their start and end apart: 1 -> 0, of which waited for: 1 -> 0; matrix products, arithmetic and copies ran while one was open for 0% -> 0% of each run, Pallas kernels for 0% -> 0%
where the time goes in v2:
time: 129 us; the launch traced here: 128 us
  Pallas kernels  107 us (83%)
  blocking collectives  11.9 us (9%)
  local copies, waits for them, and re-layouts  8.54 us (7%)
    pallas_call x1, Pallas kernels, shards(): pl.pallas_call(functools.partial(exchange_kernel, ctx_count, ch_count), i...  84.2 us
    pallas_call x1, Pallas kernels, shards(): pl.pallas_call(functools.partial(local_kernel, modes), grid=(groups,), in...  14.4 us
    all_gather x1, blocking collectives, shards(): states = lax.all_gather(state, 'ctx', axis=0)  11.9 us
    pallas_call x1, Pallas kernels, shards(): pl.pallas_call(functools.partial(gate_kernel, modes, ctx_count), grid=(gr...  8.84 us
    unnamed x3, local copies, waits for them, and re-layouts  3.87 us

profile of v2, /device:TPU:3, one launch (start us, length us, event | category | flops | bytes accessed | tf_op | source)
XLA Modules:
  0.0 127.9 jit_solution(7108434693330584245)
XLA Ops:
  0.0 1.3 %broadcast_in_dim.6.skip_ref = f32[1,1536]{1,0:T(1,128)} reshape(f32[1536]{0:T(1024)} %param.10) | data formatting | bytes 12288 | tf_op jit(solution)/shard_map/broadcast_in_dim | solution.py:277
  1.3 0.8 copy.11
  2.1 0.7 reshape.10.res_ref
  2.8 0.8 copy.10
  3.6 0.7 reshape.9.rate_ref
  4.2 1.0 broadcast_in_dim.7
  5.2 1.0 reshape.11.rates_nc_ref
  6.3 14.4 %shard_map.73 = (f32[16,1536]{1,0:T(8,128)}, f32[128,1536]{1,0:T(8,128)}) custom-call(f32[128,1536]{1,0:T(8,128)} %key_ref.3, f32[128,1536]{1,0:T(8,128)} %value_ref.3, f32[1,1536]{1,0:T(1,128)} %reshape.9.rate_ref, f32[1,1536]{1,0:T(1,128)} %reshape.10.res_ref), custom_call_target="tpu_custom_call" | custom-call | tf_op jit(solution)/shard_map/pallas_call | solution.py:257
  20.6 11.9 %all-gather = f32[128,1536]{1,0:T(8,128)} all-gather(f32[16,1536]{1,0:T(8,128)} %get-tuple-element.8), channel_id=2, replica_groups=mesh['ctx'=8,'ch'=4] {'ctx'}, dimensions={0}, use_global_device_ids=true | all-gather | bytes 884736 | tf_op jit(solution)/shard_map/all_gather | solution.py:267
  32.6 8.8 %shard_map.74.hidden_ref = bf16[128,1536]{1,0:T(8,128)(2,1)} custom-call(f32[128,1536]{1,0:T(8,128)} %query_ref.1, f32[128,1536]{1,0:T(8,128)} %key_ref.3, f32[128,1536]{1,0:T(8,128)} %value_ref.3, f32[1,1536]{1,0:T(1,128)} %broadcast_in_dim.6.skip_ref, f32[1,1536]{1,0:T(1,128)} %reshape.9.rate_ref, f32[1,1536]{1,0:T(1,128)} %reshape.10.res_ref, ...), custom_call_target="tpu_custom_call" | custom-call | tf_op jit(solution)/shard_map/pallas_call | solution.py:268
  41.4 84.2 %shard_map.75 = f32[128,2048]{1,0:T(8,128)} custom-call(bf16[128,1536]{1,0:T(8,128)(2,1)} %shard_map.74.hidden_ref, bf16[1536,1024]{1,0:T(8,128)(2,1)} %w_ref.1), custom_call_target="tpu_custom_call" | custom-call | tf_op jit(solution)/shard_map/pallas_call | solution.py:281
  125.6 2.3 %copy.13 = f32[128,2048]{1,0:T(8,128)} copy(f32[128,2048]{1,0:T(8,128)} %shard_map.75) | data formatting | bytes 2097152
